TPU v7x, 128 devices: a whole 4x4x4 slice. The times are simulated.
128 devices in a mesh: seg: 8 (over x, core), row: 16 (over z, y).
Axes of the slice: x: 4, y: 4, z: 4, core: 2. Of those that a mesh axis runs over, the one named last changes fastest.
Arguments:
- wavefunction: bfloat16 [8192, 4, 1024], P(('seg', 'row')), may hold values from -110 to 110
- left_block: bfloat16 [8192, 1024], P(('seg', 'row')), may hold values from -2 to 2, as said below
- left_edge: bfloat16 [8192, 1024], P(('seg', 'row')), may hold values from -2 to 2, as said below
- right_block: bfloat16 [8192, 1024], P('seg'), may hold values from -2 to 2, as said below
- right_edge: bfloat16 [8192, 1024], P('seg'), may hold values from -2 to 2, as said below
- fields: float32 [8, 2], P('seg'), may hold values from 0.3 to 3
- bond_values: float32 [8, 1024], P('seg'), may hold values from 0.5 to 2
- kept_rank: int32 [8], P('seg'), may hold values from 512 to 1024
Outputs:
- updated_wave: bfloat16 [8192, 4, 1024], P(('seg', 'row'))
- joined_wave: bfloat16 [8192, 4, 1024], P(('seg', 'row'))
- energies: float32 [8], P('seg')
Inputs may be any that keep to these rules, and one draw needn't show every extreme that they name: `left_block`: each segment's 1024 x 1024 block is symmetric. `left_edge`: each segment's 1024 x 1024 block is symmetric. `right_block`: each segment's 1024 x 1024 block is symmetric. `right_edge`: each segment's 1024 x 1024 block is symmetric.
All inputs are finite; a program needn't handle non-finite values.
Results may differ from a plain program's by a relative error of at most 0.006.
Values may be sent and summed in bfloat16 or wider, within the bound.
No kernel may reach another device: no remote copies, remote signals or barrier semaphores. Data moves between devices by JAX's collectives and lax.ppermute only.
A program may use at most 64 MiB of HBM per device.

v0:
```python
import jax
import jax.numpy as jnp
from jax import lax
from jax.sharding import PartitionSpec as P

STEP_SIZE = 0.25


def copy_for_each(value, axis):
    copies = jnp.broadcast_to(value, (lax.axis_size(axis), *value.shape))
    return lax.all_to_all(copies, axis, split_axis=0, concat_axis=0, tiled=True)


def over_copies(value, axis):
    everything = copy_for_each(value, axis)
    return jnp.sum(everything, axis=0)


def in_one(arrays, axis):
    ends = [0]
    for a in arrays:
        ends.append(ends[-1] + a.size)
    running = over_copies(jnp.concatenate([a.ravel() for a in arrays]), axis)
    return tuple((running[b:e].reshape(a.shape) for a, b, e in zip(arrays, ends, ends[1:])))


def split_up(value, dim, count):
    before, after = (value.shape[:dim], value.shape[dim + 1 :])
    return jnp.moveaxis(value.reshape(*before, count, -1, *after), dim, 0)


def sent_and_summed(value, axis, dim):
    parts = split_up(value, dim, lax.axis_size(axis))
    arrived = lax.all_to_all(parts, axis, split_axis=0, concat_axis=0, tiled=True)
    return arrived.sum(axis=0)


def passed_along(value, axis, steps):
    count = lax.axis_size(axis)
    first, last = (max(0, -steps), min(count, count - steps))
    return lax.ppermute(value, axis, [(source, source + steps) for source in range(first, last)])


def row_total(summands):
    return in_one((summands[0], summands[1], summands[2]), "row")


def body(
    wavefunction, left_block, left_edge, right_block, right_edge, fields, bond_values, kept_rank
):
    row_count = wavefunction.shape[0]
    bond_dim = wavefunction.shape[2]
    shard_rows = lax.all_gather(wavefunction, "row", axis=0, tiled=True)
    how_many = shard_rows.shape[0]
    rows_flat = shard_rows.reshape(how_many, 4 * bond_dim)
    left_h = jnp.dot(left_block, rows_flat, preferred_element_type=jnp.float32)
    left_z = jnp.dot(left_edge, rows_flat, preferred_element_type=jnp.float32)
    left_h = left_h.reshape(row_count, 4, bond_dim)
    left_z = left_z.reshape(row_count, 4, bond_dim)
    columns = wavefunction.reshape(row_count * 4, bond_dim)
    right_h = jnp.dot(columns, right_block, preferred_element_type=jnp.float32).reshape(
        row_count, 4, bond_dim
    )
    right_z = jnp.dot(columns, right_edge, preferred_element_type=jnp.float32).reshape(
        row_count, 4, bond_dim
    )
    sign_one = jnp.array([1.0, 1.0, -1.0, -1.0], jnp.float32).reshape(1, 4, 1)
    sign_two = jnp.array([1.0, -1.0, 1.0, -1.0], jnp.float32).reshape(1, 4, 1)
    values = wavefunction.astype(jnp.float32)
    swap_one = jnp.concatenate([values[:, 2:4], values[:, 0:2]], 1)
    swap_two = jnp.stack([values[:, 1], values[:, 0], values[:, 3], values[:, 2]], 1)
    field_pair = fields[0]
    applied = (
        left_h
        + sign_one * left_z
        + right_h
        + sign_two * right_z
        - sign_one * sign_two * values
        - field_pair[0] * swap_one
        - field_pair[1] * swap_two
    )
    squares_local = jnp.sum(values * values)
    rayleigh_local = jnp.sum(values * applied)
    squares, rayleigh, image_square = row_total(
        (squares_local, rayleigh_local, jnp.sum(applied * applied))
    )
    energy = rayleigh / squares
    stepped = values - STEP_SIZE * (applied - energy * values)
    renorm = squares + STEP_SIZE * STEP_SIZE * (image_square - rayleigh * rayleigh / squares)
    wave_new = (stepped * jnp.sqrt(bond_dim / renorm)).astype(jnp.bfloat16)
    new_columns = wave_new.reshape(row_count * 4, bond_dim)
    gram = sent_and_summed(
        lax.dot_general(
            new_columns, new_columns, (((0,), (0,)), ((), ())), preferred_element_type=jnp.float32
        ),
        "row",
        0,
    )
    offset = lax.axis_index("row") * row_count
    positions = jnp.arange(bond_dim)
    inverse = jnp.where(positions < kept_rank[0], 1.0 / bond_values[0], 0.0)
    inverse_rows = lax.dynamic_slice_in_dim(inverse, offset, row_count, 0)
    weighted = (inverse_rows[:, None] * gram * inverse[None, :]).astype(jnp.bfloat16)
    previous = passed_along(weighted, "seg", 1)
    shard_rows = lax.all_gather(wave_new, "row", axis=0, tiled=True)
    how_many = shard_rows.shape[0]
    joined = jnp.dot(
        previous, shard_rows.reshape(how_many, 4 * bond_dim), preferred_element_type=jnp.float32
    )
    joined_wave = joined.astype(jnp.bfloat16).reshape(row_count, 4, bond_dim)
    return (wave_new, joined_wave, energy.reshape(1))


def solution(mesh):
    in_specs = (
        P(("seg", "row"), None, None),
        P(("seg", "row"), None),
        P(("seg", "row"), None),
        P("seg", None),
        P("seg", None),
        P("seg", None),
        P("seg", None),
        P("seg"),
    )
    out_specs = (P(("seg", "row"), None, None), P(("seg", "row"), None, None), P("seg"))
    return jax.shard_map(body, mesh=mesh, in_specs=in_specs, out_specs=out_specs, check_vma=False)
```

profile of v0, /device:TPU:1, one launch (start us, length us, event | category | flops | bytes accessed | tf_op | source)
XLA Modules:
  0.0 274.9 jit_solution(6586143170617328613)
XLA Ops:
  7.2 0.0 copy-start
  7.2 0.0 all-gather.3.cloned.1.call-start
  7.2 0.7 all-gather.3.cloned.1.call-update
  7.9 0.0 all-gather.5.cloned.1.call-start
  8.0 1.3 fusion.46
  9.3 1.2 copy_convert_fusion
  10.5 0.9 fusion.43
  11.4 0.9 fusion.44
  12.3 3.4 %fusion.20 = f32[64,4,1024]{2,0,1:T(8,128)} fusion(bf16[1024,1024]{1,0:T(8,128)(2,1)} %param.14, f32[4]{0:T(128)} %constant.25.clone, bf16[64,4,1024]{2,1,0:T(4,128)(2,1)} %param.10), kind=kOutput, calls=%fused_computation.13 | convolution fusion | flops 537133056 | bytes 3670032 | tf_op jit(solution)/shard_map/dot_general | solution.py:64
  15.7 0.0 copy-start.9
  15.7 0.0 copy-start.11
  15.7 68.5 %all-gather.3.cloned.1.call-done = bf16[1024,4,1024]{2,1,0:T(4,128)(2,1)} async-done(((bf16[64,4,1024]{2,1,0:T(4,128)(2,1)}), bf16[1024,4,1024]{2,1,0:T(4,128)(2,1)}) %all-gather.3.cloned.1.call-update) | async-done | bytes 8388624 | tf_op jit(solution)/shard_map/all_gather | solution.py:53
  84.1 13.7 %copy.60 = bf16[1024,4,1024]{0,2,1:T(8,128)(2,1)} copy(bf16[1024,4,1024]{2,1,0:T(4,128)(2,1)} %all-gather.3.cloned.1.call-done) | data formatting | bytes 16777216 | tf_op jit(solution)/shard_map/reshape | solution.py:55
  97.8 0.0 copy-done.9
  97.8 0.0 copy-done.11
  97.8 0.0 copy-start.1
  97.9 0.0 copy-start.2
  97.9 0.0 copy-start.4
  97.9 0.0 copy-start.5
  97.9 0.0 copy-start.6
  97.9 0.0 copy-start.7
  97.9 0.0 copy-start.8
  97.9 0.0 copy-start.12
  97.9 6.2 %fusion.29 = f32[64,4,1024]{2,0,1:T(8,128)S(1)} fusion(bf16[1024,4,1024]{0,2,1:T(8,128)(2,1)} %copy.60, f32[4]{0:T(128)S(1)} %copy-done.11, bf16[64,1024]{1,0:T(8,128)(2,1)S(1)} %copy-done.9), kind=kOutput, calls=%fused_computation.21 | convolution fusion | flops 537133056 | bytes 9568272 | tf_op jit(solution)/shard_map/dot_general | solution.py:57
  104.1 0.0 copy-done.1
  104.1 3.6 %fusion.26 = f32[64,4,1024]{2,0,1:T(8,128)S(1)} fusion(f32[64,4,1024]{2,0,1:T(8,128)S(1)} %fusion.29, bf16[1024,4,1024]{0,2,1:T(8,128)(2,1)S(1)} %copy-done.1, bf16[64,1024]{1,0:T(8,128)(2,1)} %param.11), kind=kOutput, calls=%fused_computation.20 | convolution fusion | flops 537133056 | bytes 10616832 | tf_op jit(solution)/shard_map/dot_general | solution.py:56
  107.7 0.0 copy-done
  107.7 0.0 copy-done.2
  107.7 0.0 copy-done.4
  107.7 0.0 copy-done.5
  107.7 0.0 copy-done.6
  107.7 0.0 copy-done.7
  107.7 0.0 copy-done.8
  107.8 0.0 copy-done.12
  107.8 4.0 %fusion.33 = (f32[]{:T(128)}, f32[]{:T(128)}, f32[]{:T(128)}, f32[64,4,1024]{2,0,1:T(8,128)}) fusion(bf16[64,4,1024]{2,1,0:T(4,128)(2,1)S(1)} %copy-done.2, f32[64,1,1024]{2,0,1:T(8,128)S(1)} %copy-done.8, f32[64,1,1024]{2,0,1:T(8,128)S(1)} %copy-done.6, f32[64,1,1024]{2,0,1:T(8,128)S(1)} %copy-done.7, f32[64,1,1024]{2,0,1:T(8,128)S(1)} %get-tuple-element.26, ...), kind=kOutput, calls=%fused_computation.23 | convolution fusion | flops 541851648 | bytes 7864356 | tf_op jit(solution)/shard_map/dot_general | solution.py:61
  111.8 1.9 pad_maximum_fusion
  113.8 11.2 %all_to_all.11 = f32[16,1,3]{2,1,0:T(1,128)S(1)} all-to-all(f32[16,1,3]{2,1,0:T(1,128)S(1)} %broadcast_in_dim.11), channel_id=1, replica_groups=mesh['seg'=8,'row'=16] {'row'}, dimensions={0} | all-to-all | bytes 384 | tf_op jit(solution)/shard_map/all_to_all | solution.py:11
  125.0 0.6 fusion.45
  130.3 2.3 fusion.37
  132.6 0.0 all-gather.5.cloned.1.call-update
  132.6 1.5 copy.59
  134.1 0.0 copy-start.3
  134.1 0.0 copy-start.10
  134.1 0.1 reshape.91
  134.2 1.0 reshape.83
  135.2 2.1 copy.57
  137.3 3.7 %fusion.47 = f32[16,64,1024]{2,1,0:T(8,128)} fusion(bf16[16,64,256]{2,1,0:T(8,128)(2,1)} %bitcast.61, bf16[256,1024,1]{1,0,2:T(8,128)(2,1)S(1)} %reshape.91), kind=kOutput, calls=%fused_computation.46 | convolution fusion | flops 536870912 | bytes 5242880 | tf_op jit(solution)/shard_map/dot_general | solution.py:93
  141.0 0.0 copy-done.3
  141.0 4.6 %all-to-all-start.1 = ((f32[16,64,1024]{2,1,0:T(8,128)}), f32[16,64,1024]{2,1,0:T(8,128)}, u32[]{:S(2)}, u32[]{:S(2)}) async-start(f32[16,64,1024]{2,1,0:T(8,128)} %fusion.47), calls=%async_computation.1 | async-start | bytes 8388608 | tf_op jit(solution)/shard_map/all_to_all | solution.py:34
  146.2 0.0 copy-done.10
  146.3 0.1 dynamic_slice.3
  146.4 67.0 %all-to-all-done.1 = f32[16,64,1024]{2,1,0:T(8,128)} async-done(((f32[16,64,1024]{2,1,0:T(8,128)}), f32[16,64,1024]{2,1,0:T(8,128)}, u32[]{:S(2)}, u32[]{:S(2)}) %all-to-all-start.1) | async-done | bytes 4194336 | tf_op jit(solution)/shard_map/all_to_all | solution.py:34
  213.4 2.5 reduce_sum.49
  215.9 0.1 multiply_convert_fusion
  216.0 5.8 %collective-permute-start = (bf16[64,1024]{1,0:T(8,128)(2,1)S(1)}, bf16[64,1024]{1,0:T(8,128)(2,1)S(1)}, u32[]{:S(2)}, u32[]{:S(2)}) collective-permute-start(bf16[64,1024]{1,0:T(8,128)(2,1)S(1)} %multiply_convert_fusion), channel_id=1, source_target_pairs={{0,16},{16,32},{32,48},{48,64},{64,80},{80,96},{96,112},{1,17},{17... | collective-permute-start | bytes 393224 | tf_op jit(solution)/shard_map/ppermute | solution.py:41
  221.8 26.5 %all-gather.5.cloned.1.call-done = bf16[1024,4,1024]{2,0,1:T(8,128)(2,1)} async-done(((bf16[64,4,1024]{2,0,1:T(8,128)(2,1)}), bf16[1024,4,1024]{2,0,1:T(8,128)(2,1)}) %all-gather.5.cloned.1.call-update) | async-done | bytes 8388624 | tf_op jit(solution)/shard_map/all_gather | solution.py:105
  248.3 11.4 %copy.58 = bf16[1024,4,1024]{0,2,1:T(8,128)(2,1)} copy(bf16[1024,4,1024]{2,0,1:T(8,128)(2,1)} %all-gather.5.cloned.1.call-done) | data formatting | bytes 16777216 | tf_op jit(solution)/shard_map/all_gather | solution.py:105
  259.7 0.0 collective-permute-done
  259.7 6.0 %convolution_convert_fusion = bf16[64,4096]{1,0:T(8,128)(2,1)S(1)} fusion(bf16[64,1024]{1,0:T(8,128)(2,1)S(1)} %collective-permute-done, bf16[1024,4096]{0,1:T(8,128)(2,1)} %bitcast.60), kind=kOutput, calls=%fused_computation.4 | convolution fusion | flops 537133056 | bytes 9043968 | tf_op jit(solution)/shard_map/dot_general | solution.py:107
  265.7 1.2 reshape.85
  (4 shorter events, 0.1 us)
Async XLA Ops:
  7.2 100.5 %copy-start = (bf16[1024,1024]{1,0:T(8,128)(2,1)S(1)}, bf16[1024,1024]{1,0:T(8,128)(2,1)}, u32[]{:S(2)}) copy-start(bf16[1024,1024]{1,0:T(8,128)(2,1)} %param.13) | copy-start | bytes 6291460
  7.2 77.0 %all-gather.3.cloned.1.call-start = ((), (), s32[]{:S(2)}) async-start(), calls=%async_computation.2 | async-start | bytes 8912896 | tf_op jit(solution)/shard_map/all_gather | solution.py:53
  7.9 240.4 %all-gather.5.cloned.1.call-start = ((), (), s32[]{:S(2)}) async-start(), calls=%async_computation.3 | async-start | bytes 8912896 | tf_op jit(solution)/shard_map/all_gather | solution.py:105
  15.7 82.2 %copy-start.9 = (bf16[64,1024]{1,0:T(8,128)(2,1)S(1)}, bf16[64,1024]{1,0:T(8,128)(2,1)}, u32[]{:S(2)}) copy-start(bf16[64,1024]{1,0:T(8,128)(2,1)} %param.12) | copy-start | bytes 393220
  15.7 82.2 %copy-start.11 = (f32[4]{0:T(128)S(1)}, f32[4]{0:T(128)}, u32[]{:S(2)}) copy-start(f32[4]{0:T(128)} %constant.24.clone) | copy-start | bytes 52
  97.8 6.3 %copy-start.1 = (bf16[1024,4,1024]{0,2,1:T(8,128)(2,1)S(1)}, bf16[1024,4,1024]{0,2,1:T(8,128)(2,1)}, u32[]{:S(2)}) copy-start(bf16[1024,4,1024]{0,2,1:T(8,128)(2,1)} %copy.60) | copy-start | bytes 25165828
  97.9 9.9 %copy-start.2 = (bf16[64,4,1024]{2,1,0:T(4,128)(2,1)S(1)}, bf16[64,4,1024]{2,1,0:T(4,128)(2,1)}, u32[]{:S(2)}) copy-start(bf16[64,4,1024]{2,1,0:T(4,128)(2,1)} %param.10) | copy-start | bytes 1572868
  97.9 9.8 %copy-start.4 = (f32[64,4,1024]{2,0,1:T(8,128)S(1)}, f32[64,4,1024]{2,0,1:T(8,128)}, u32[]{:S(2)}) copy-start(f32[64,4,1024]{2,0,1:T(8,128)} %fusion.20) | copy-start | bytes 3145732
  97.9 9.8 %copy-start.5 = (f32[64,2,1024]{2,0,1:T(8,128)S(1)}, f32[64,2,1024]{2,0,1:T(8,128)}, u32[]{:S(2)}) copy-start(f32[64,2,1024]{2,0,1:T(8,128)} %get-tuple-element.31) | copy-start | bytes 1572868
  97.9 9.8 %copy-start.6 = (f32[64,1,1024]{2,0,1:T(8,128)S(1)}, f32[64,1,1024]{2,0,1:T(8,128)}, u32[]{:S(2)}) copy-start(f32[64,1,1024]{2,0,1:T(8,128)} %get-tuple-element.27) | copy-start | bytes 786436
  97.9 9.8 %copy-start.7 = (f32[64,1,1024]{2,0,1:T(8,128)S(1)}, f32[64,1,1024]{2,0,1:T(8,128)}, u32[]{:S(2)}) copy-start(f32[64,1,1024]{2,0,1:T(8,128)} %get-tuple-element.28) | copy-start | bytes 786436
  97.9 9.8 %copy-start.8 = (f32[64,1,1024]{2,0,1:T(8,128)S(1)}, f32[64,1,1024]{2,0,1:T(8,128)}, u32[]{:S(2)}) copy-start(f32[64,1,1024]{2,0,1:T(8,128)} %get-tuple-element.29) | copy-start | bytes 786436
  97.9 9.8 %copy-start.12 = (f32[4]{0:T(128)S(1)}, f32[4]{0:T(128)}, u32[]{:S(2)}) copy-start(f32[4]{0:T(128)} %constant.32) | copy-start | bytes 52
  134.1 6.9 %copy-start.3 = (bf16[64,4,1024]{2,1,0:T(4,128)(2,1)}, bf16[64,4,1024]{2,1,0:T(4,128)(2,1)S(1)}, u32[]{:S(2)}) copy-start(bf16[64,4,1024]{2,1,0:T(4,128)(2,1)S(1)} %copy.59) | copy-start | bytes 1572868
  134.1 12.1 %copy-start.10 = (f32[1,1024]{1,0:T(1,128)S(1)}, f32[1,1024]{1,0:T(1,128)}, u32[]{:S(2)}) copy-start(f32[1,1024]{1,0:T(1,128)} %param.16) | copy-start | bytes 12292
  141.0 72.4 %all-to-all-start.1 = ((f32[16,64,1024]{2,1,0:T(8,128)}), f32[16,64,1024]{2,1,0:T(8,128)}, u32[]{:S(2)}, u32[]{:S(2)}) async-start(f32[16,64,1024]{2,1,0:T(8,128)} %fusion.47), calls=%async_computation.1 | async-start | bytes 8388608 | tf_op jit(solution)/shard_map/all_to_all | solution.py:34
  216.0 43.7 %collective-permute-start = (bf16[64,1024]{1,0:T(8,128)(2,1)S(1)}, bf16[64,1024]{1,0:T(8,128)(2,1)S(1)}, u32[]{:S(2)}, u32[]{:S(2)}) collective-permute-start(bf16[64,1024]{1,0:T(8,128)(2,1)S(1)} %multiply_convert_fusion), channel_id=1, source_target_pairs={{0,16},{16,32},{32,48},{48,64},{64,80},{80,96},{96,112},{1,17},{17... | collective-permute-start | bytes 393224 | tf_op jit(solution)/shard_map/ppermute | solution.py:41
Sparse Core Ops, SparseCore 0:
  10.1 73.9 all-gather.2
  132.8 115.4 all-gather.4
where the time goes:
time: 276 us; the launch traced here: 275 us
  waiting for transfers between devices  163 us (59%)
  local copies, waits for them, and re-layouts  34.8 us (13%)
  matrix products  26.9 us (10%)
  between operations  20.7 us (8%)
  blocking collectives  11.2 us (4%)
  starting transfers between devices  10.4 us (4%)
  other arithmetic  8.08 us (3%)
    all_gather x1, waiting for transfers between devices, body(): shard_rows = lax.all_gather(wavefunction, 'row', axis=0, tiled=True)  68.5 us
    all_to_all x1, waiting for transfers between devices, sent_and_summed(): lax.all_to_all(parts, axis, split_axis=0, concat_axis=0, tiled=True)  67 us
    all_gather x1, waiting for transfers between devices, body(): shard_rows = lax.all_gather(wave_new, 'row', axis=0, tiled=True)  26.5 us
    reshape x1, local copies, waits for them, and re-layouts, body(): rows_flat = shard_rows.reshape(how_many, 4 * bond_dim)  13.7 us
    all_gather x1, local copies, waits for them, and re-layouts, body(): shard_rows = lax.all_gather(wave_new, 'row', axis=0, tiled=True)  11.4 us
    all_to_all x1, blocking collectives, copy_for_each(): return lax.all_to_all(copies, axis, split_axis=0, concat_axis=0, tiled=True)  11.2 us
    dot_general x1, matrix products, body(): left_z = jnp.dot(left_edge, rows_flat, preferred_element_type=jnp.float32)  6.19 us
    dot_general x1, matrix products, body(): jnp.dot(previous, shard_rows.reshape(how_many, 4 * bond_dim), preferred_e...  6.04 us
  transfers between devices with their start and end apart: 4, of which 3 were waited for; matrix products, arithmetic and copies ran while one was open for 11% of the time, Pallas kernels for 0%

commit v1 on v0

--- a/solution.py
+++ b/solution.py
@@ -102,7 +102,8 @@
     inverse_rows = lax.dynamic_slice_in_dim(inverse, offset, row_count, 0)
     weighted = (inverse_rows[:, None] * gram * inverse[None, :]).astype(jnp.bfloat16)
     previous = passed_along(weighted, "seg", 1)
-    shard_rows = lax.all_gather(wave_new, "row", axis=0, tiled=True)
+    repeated = jnp.stack([wave_new] * lax.axis_size("row"))
+    shard_rows = jnp.concatenate(lax.all_to_all(repeated, "row", 0, 0), axis=0)
     how_many = shard_rows.shape[0]
     joined = jnp.dot(
         previous, shard_rows.reshape(how_many, 4 * bond_dim), preferred_element_type=jnp.float32

time: 276 us -> 351 us (1.27)
  blocking collectives: 11.2 us -> 64.5 us
  waiting for transfers between devices: 163 us -> 178 us
  local copies, waits for them, and re-layouts: 34.8 us -> 41.2 us
    all_to_all x0 -> x1, blocking collectives: none -> 53.3 us  [sent_and_summed(): lax.all_to_all(parts, axis, split_axis=0, concat_axis=0, tiled=True)]
    all_to_all x1, waiting for transfers between devices: 67 us -> 109 us  [body(): shard_rows = jnp.concatenate(lax.all_to_all(repeated, 'row', 0, 0), axis=0)]
    all_gather x1 -> x0, waiting for transfers between devices: 26.5 us -> none  [body(): shard_rows = lax.all_gather(wave_new, 'row', axis=0, tiled=True)]
    all_gather x1 -> x0, local copies, waits for them, and re-layouts: 11.4 us -> none  [body(): shard_rows = lax.all_gather(wave_new, 'row', axis=0, tiled=True)]
    unnamed x27 -> x28, local copies, waits for them, and re-layouts: 1.52 us -> 12.6 us
    another operation x0 -> x1, local copies, waits for them, and re-layouts: none -> 6.75 us  [body(): repeated = jnp.stack([wave_new] * lax.axis_size('row'))]
  transfers between devices with their start and end apart: 4 -> 3, of which waited for: 3 -> 2; matrix products, arithmetic and copies ran while one was open for 11% -> 7% of each run, Pallas kernels for 0% -> 0%
where the time goes in v1:
time: 351 us; the launch traced here: 347 us
  waiting for transfers between devices  178 us (51%)
  blocking collectives  64.5 us (18%)
  local copies, waits for them, and re-layouts  41.2 us (12%)
  matrix products  24 us (7%)
  between operations  20.7 us (6%)
  starting transfers between devices  11.2 us (3%)
  other arithmetic  7.35 us (2%)
    all_to_all x1, waiting for transfers between devices, body(): shard_rows = jnp.concatenate(lax.all_to_all(repeated, 'row', 0, 0), axis=0)  109 us
    all_gather x1, waiting for transfers between devices, body(): shard_rows = lax.all_gather(wavefunction, 'row', axis=0, tiled=True)  68.4 us
    all_to_all x1, blocking collectives, sent_and_summed(): lax.all_to_all(parts, axis, split_axis=0, concat_axis=0, tiled=True)  53.3 us
    reshape x1, local copies, waits for them, and re-layouts, body(): rows_flat = shard_rows.reshape(how_many, 4 * bond_dim)  13.7 us
    unnamed x28, local copies, waits for them, and re-layouts  12.6 us
    all_to_all x1, blocking collectives, copy_for_each(): return lax.all_to_all(copies, axis, split_axis=0, concat_axis=0, tiled=True)  11.2 us
  transfers between devices with their start and end apart: 3, of which 2 were waited for; matrix products, arithmetic and copies ran while one was open for 7% of the time, Pallas kernels for 0%

profile of v1, /device:TPU:1, one launch (start us, length us, event | category | flops | bytes accessed | tf_op | source)
XLA Modules:
  0.0 347.3 jit_solution(4285687756170507353)
XLA Ops:
  7.2 0.0 copy-start
  7.2 0.0 all-gather.2.cloned.1.call-start
  7.2 0.7 all-gather.2.cloned.1.call-update
  7.9 1.4 fusion.46
  9.3 1.2 copy_convert_fusion
  10.5 0.9 fusion.43
  11.4 0.9 fusion.44
  12.3 3.4 fusion.20
  15.7 0.0 copy-start.9
  15.7 0.0 copy-start.11
  15.7 68.4 %all-gather.2.cloned.1.call-done = bf16[1024,4,1024]{2,1,0:T(4,128)(2,1)} async-done(((bf16[64,4,1024]{2,1,0:T(4,128)(2,1)}), bf16[1024,4,1024]{2,1,0:T(4,128)(2,1)}) %all-gather.2.cloned.1.call-update) | async-done | bytes 8388624 | tf_op jit(solution)/shard_map/all_gather | solution.py:53
  84.1 13.7 %copy.61 = bf16[1024,4,1024]{0,2,1:T(8,128)(2,1)} copy(bf16[1024,4,1024]{2,1,0:T(4,128)(2,1)} %all-gather.2.cloned.1.call-done) | data formatting | bytes 16777216 | tf_op jit(solution)/shard_map/reshape | solution.py:55
  97.9 0.0 copy-done.9
  97.9 0.0 copy-done.11
  97.9 0.0 copy-start.1
  97.9 0.0 copy-start.2
  97.9 0.0 copy-start.4
  97.9 0.0 copy-start.5
  97.9 0.0 copy-start.6
  97.9 0.0 copy-start.7
  97.9 0.0 copy-start.8
  97.9 0.0 copy-start.12
  97.9 6.2 %fusion.29 = f32[64,4,1024]{2,0,1:T(8,128)S(1)} fusion(bf16[1024,4,1024]{0,2,1:T(8,128)(2,1)} %copy.61, f32[4]{0:T(128)S(1)} %copy-done.11, bf16[64,1024]{1,0:T(8,128)(2,1)S(1)} %copy-done.9), kind=kOutput, calls=%fused_computation.21 | convolution fusion | flops 537133056 | bytes 9568272 | tf_op jit(solution)/shard_map/dot_general | solution.py:57
  104.1 0.0 copy-done.1
  104.1 3.6 %fusion.26 = f32[64,4,1024]{2,0,1:T(8,128)S(1)} fusion(f32[64,4,1024]{2,0,1:T(8,128)S(1)} %fusion.29, bf16[1024,4,1024]{0,2,1:T(8,128)(2,1)S(1)} %copy-done.1, bf16[64,1024]{1,0:T(8,128)(2,1)} %param.11), kind=kOutput, calls=%fused_computation.20 | convolution fusion | flops 537133056 | bytes 10616832 | tf_op jit(solution)/shard_map/dot_general | solution.py:56
  107.7 0.0 copy-done
  107.7 0.0 copy-done.2
  107.7 0.0 copy-done.4
  107.7 0.0 copy-done.5
  107.7 0.0 copy-done.6
  107.8 0.0 copy-done.7
  107.8 0.0 copy-done.8
  107.8 0.0 copy-done.12
  107.8 4.2 %fusion.33 = (f32[]{:T(128)}, f32[]{:T(128)}, f32[]{:T(128)}, f32[64,4,1024]{2,0,1:T(8,128)}) fusion(bf16[64,4,1024]{2,1,0:T(4,128)(2,1)S(1)} %copy-done.2, f32[64,1,1024]{2,0,1:T(8,128)S(1)} %copy-done.8, f32[64,1,1024]{2,0,1:T(8,128)S(1)} %copy-done.6, f32[64,1,1024]{2,0,1:T(8,128)S(1)} %copy-done.7, f32[64,1,1024]{2,0,1:T(8,128)S(1)} %get-tuple-element.26, ...), kind=kOutput, calls=%fused_computation.23 | convolution fusion | flops 541851648 | bytes 7864356 | tf_op jit(solution)/shard_map/dot_general | solution.py:61
  112.0 2.0 pad_maximum_fusion
  114.0 11.2 %all_to_all.16 = f32[16,1,3]{2,1,0:T(1,128)S(1)} all-to-all(f32[16,1,3]{2,1,0:T(1,128)S(1)} %broadcast_in_dim.11), channel_id=1, replica_groups=mesh['seg'=8,'row'=16] {'row'}, dimensions={0} | all-to-all | bytes 384 | tf_op jit(solution)/shard_map/all_to_all | solution.py:11
  125.3 0.6 fusion.45
  130.5 1.5 fusion.37
  132.1 0.4 copy.60
  132.5 0.0 copy-start.3
  132.5 0.1 reshape.89
  132.6 0.9 reshape.82
  133.5 2.0 copy.58
  135.6 1.7 fusion.47
  137.3 53.3 %all_to_all.17 = f32[16,64,1024]{2,1,0:T(8,128)} all-to-all(f32[16,64,1024]{2,1,0:T(8,128)S(1)} %fusion.47), channel_id=1, replica_groups=mesh['seg'=8,'row'=16] {'row'}, dimensions={0} | all-to-all | bytes 8388608 | tf_op jit(solution)/shard_map/all_to_all | solution.py:34
  190.6 0.0 copy-done.3
  190.6 6.7 %stack.5 = bf16[16,64,4,1024]{3,2,1,0:T(4,128)(2,1)} broadcast(bf16[64,4,1024]{2,1,0:T(4,128)(2,1)S(1)} %copy.60), dimensions={1,2,3} | broadcast | bytes 8912896 | tf_op jit(solution)/shard_map/stack | solution.py:105
  197.3 0.0 copy-start.10
  197.3 5.1 %all-to-all-start.2 = ((bf16[16,64,4,1024]{3,2,1,0:T(4,128)(2,1)}), bf16[16,64,4,1024]{3,2,1,0:T(4,128)(2,1)}, u32[]{:S(2)}, u32[]{:S(2)}) async-start(bf16[16,64,4,1024]{3,2,1,0:T(4,128)(2,1)} %stack.5), calls=%async_computation.2 | async-start | bytes 16777216 | tf_op jit(solution)/shard_map/all_to_all | solution.py:106
  203.0 0.0 copy-done.10
  203.1 0.1 dynamic_slice.3
  203.2 2.5 reduce_sum.49
  205.7 0.1 multiply_convert_fusion
  205.8 6.1 %collective-permute-start = (bf16[64,1024]{1,0:T(8,128)(2,1)S(1)}, bf16[64,1024]{1,0:T(8,128)(2,1)S(1)}, u32[]{:S(2)}, u32[]{:S(2)}) collective-permute-start(bf16[64,1024]{1,0:T(8,128)(2,1)S(1)} %multiply_convert_fusion), channel_id=1, source_target_pairs={{0,16},{16,32},{32,48},{48,64},{64,80},{80,96},{96,112},{1,17},{17... | collective-permute-start | bytes 393224 | tf_op jit(solution)/shard_map/ppermute | solution.py:41
  211.9 109.2 %all-to-all-done.2 = bf16[16,64,4,1024]{3,2,1,0:T(4,128)(2,1)} async-done(((bf16[16,64,4,1024]{3,2,1,0:T(4,128)(2,1)}), bf16[16,64,4,1024]{3,2,1,0:T(4,128)(2,1)}, u32[]{:S(2)}, u32[]{:S(2)}) %all-to-all-start.2) | async-done | bytes 8388640 | tf_op jit(solution)/shard_map/all_to_all | solution.py:106
  321.1 12.1 %copy.66 = bf16[128,8,4,1024]{3,1,2,0:T(8,128)(2,1)} copy(bf16[128,8,4,1024]{3,2,1,0:T(4,128)(2,1)} %bitcast.24) | data formatting | bytes 16777216
  333.2 0.0 collective-permute-done
  333.2 4.9 %convolution_convert_fusion = bf16[64,4096]{1,0:T(8,128)(2,1)S(1)} fusion(bf16[64,1024]{1,0:T(8,128)(2,1)S(1)} %collective-permute-done, bf16[1024,4096]{1,0:T(8,128)(2,1)} %bitcast.62), kind=kOutput, calls=%fused_computation.4 | convolution fusion | flops 537133056 | bytes 9043968 | tf_op jit(solution)/shard_map/dot_general | solution.py:108
  338.2 1.2 reshape.83
  (4 shorter events, 0.1 us)
Async XLA Ops:
  7.2 100.5 %copy-start = (bf16[1024,1024]{1,0:T(8,128)(2,1)S(1)}, bf16[1024,1024]{1,0:T(8,128)(2,1)}, u32[]{:S(2)}) copy-start(bf16[1024,1024]{1,0:T(8,128)(2,1)} %param.13) | copy-start | bytes 6291460
  7.2 77.0 %all-gather.2.cloned.1.call-start = ((), (), s32[]{:S(2)}) async-start(), calls=%async_computation.3 | async-start | bytes 8912896 | tf_op jit(solution)/shard_map/all_gather | solution.py:53
  15.7 82.1 %copy-start.9 = (bf16[64,1024]{1,0:T(8,128)(2,1)S(1)}, bf16[64,1024]{1,0:T(8,128)(2,1)}, u32[]{:S(2)}) copy-start(bf16[64,1024]{1,0:T(8,128)(2,1)} %param.12) | copy-start | bytes 393220
  15.7 82.2 %copy-start.11 = (f32[4]{0:T(128)S(1)}, f32[4]{0:T(128)}, u32[]{:S(2)}) copy-start(f32[4]{0:T(128)} %constant.24.clone) | copy-start | bytes 52
  97.9 6.3 %copy-start.1 = (bf16[1024,4,1024]{0,2,1:T(8,128)(2,1)S(1)}, bf16[1024,4,1024]{0,2,1:T(8,128)(2,1)}, u32[]{:S(2)}) copy-start(bf16[1024,4,1024]{0,2,1:T(8,128)(2,1)} %copy.61) | copy-start | bytes 25165828
  97.9 9.9 %copy-start.2 = (bf16[64,4,1024]{2,1,0:T(4,128)(2,1)S(1)}, bf16[64,4,1024]{2,1,0:T(4,128)(2,1)}, u32[]{:S(2)}) copy-start(bf16[64,4,1024]{2,1,0:T(4,128)(2,1)} %param.10) | copy-start | bytes 1572868
  97.9 9.8 %copy-start.4 = (f32[64,4,1024]{2,0,1:T(8,128)S(1)}, f32[64,4,1024]{2,0,1:T(8,128)}, u32[]{:S(2)}) copy-start(f32[64,4,1024]{2,0,1:T(8,128)} %fusion.20) | copy-start | bytes 3145732
  97.9 9.8 %copy-start.5 = (f32[64,2,1024]{2,0,1:T(8,128)S(1)}, f32[64,2,1024]{2,0,1:T(8,128)}, u32[]{:S(2)}) copy-start(f32[64,2,1024]{2,0,1:T(8,128)} %get-tuple-element.31) | copy-start | bytes 1572868
  97.9 9.8 %copy-start.6 = (f32[64,1,1024]{2,0,1:T(8,128)S(1)}, f32[64,1,1024]{2,0,1:T(8,128)}, u32[]{:S(2)}) copy-start(f32[64,1,1024]{2,0,1:T(8,128)} %get-tuple-element.27) | copy-start | bytes 786436
  97.9 9.8 %copy-start.7 = (f32[64,1,1024]{2,0,1:T(8,128)S(1)}, f32[64,1,1024]{2,0,1:T(8,128)}, u32[]{:S(2)}) copy-start(f32[64,1,1024]{2,0,1:T(8,128)} %get-tuple-element.28) | copy-start | bytes 786436
  97.9 9.8 %copy-start.8 = (f32[64,1,1024]{2,0,1:T(8,128)S(1)}, f32[64,1,1024]{2,0,1:T(8,128)}, u32[]{:S(2)}) copy-start(f32[64,1,1024]{2,0,1:T(8,128)} %get-tuple-element.29) | copy-start | bytes 786436
  97.9 9.8 %copy-start.12 = (f32[4]{0:T(128)S(1)}, f32[4]{0:T(128)}, u32[]{:S(2)}) copy-start(f32[4]{0:T(128)} %constant.32) | copy-start | bytes 52
  132.5 58.1 %copy-start.3 = (bf16[64,4,1024]{2,1,0:T(4,128)(2,1)}, bf16[64,4,1024]{2,1,0:T(4,128)(2,1)S(1)}, u32[]{:S(2)}) copy-start(bf16[64,4,1024]{2,1,0:T(4,128)(2,1)S(1)} %copy.60) | copy-start | bytes 1572868
  197.3 5.7 %copy-start.10 = (f32[1,1024]{1,0:T(1,128)S(1)}, f32[1,1024]{1,0:T(1,128)}, u32[]{:S(2)}) copy-start(f32[1,1024]{1,0:T(1,128)} %param.16) | copy-start | bytes 12292
  197.3 123.7 %all-to-all-start.2 = ((bf16[16,64,4,1024]{3,2,1,0:T(4,128)(2,1)}), bf16[16,64,4,1024]{3,2,1,0:T(4,128)(2,1)}, u32[]{:S(2)}, u32[]{:S(2)}) async-start(bf16[16,64,4,1024]{3,2,1,0:T(4,128)(2,1)} %stack.5), calls=%async_computation.2 | async-start | bytes 16777216 | tf_op jit(solution)/shard_map/all_to_all | solution.py:106
  205.8 127.4 %collective-permute-start = (bf16[64,1024]{1,0:T(8,128)(2,1)S(1)}, bf16[64,1024]{1,0:T(8,128)(2,1)S(1)}, u32[]{:S(2)}, u32[]{:S(2)}) collective-permute-start(bf16[64,1024]{1,0:T(8,128)(2,1)S(1)} %multiply_convert_fusion), channel_id=1, source_target_pairs={{0,16},{16,32},{32,48},{48,64},{64,80},{80,96},{96,112},{1,17},{17... | collective-permute-start | bytes 393224 | tf_op jit(solution)/shard_map/ppermute | solution.py:41
Sparse Core Ops, SparseCore 0:
  10.1 73.9 all-gather.1
